TPU v7x, 512 devices: a whole 4x8x8 slice. The times are simulated.
512 devices in a mesh: grp: 8 (over y), sp: 64 (over x, z, core).
Axes of the slice: x: 4, y: 8, z: 8, core: 2. Of those that a mesh axis runs over, the one named last changes fastest.
Arguments:
- snapshots: float32 [3, 8192, 24576], P(None, 'grp', 'sp'), may hold values from -12 to 12
- kept_bins: int32 [64], replicated, may hold values from 1 to 255, as said below
- weights: float32 [24576], P('sp'), may hold values from 0.1 to 80
Outputs:
- mode_fields: float32 [2, 64, 4, 3, 24576], P(None, 'grp', None, None, 'sp')
- energies: float32 [64, 4], P('grp')
Inputs may be any that keep to these rules, and one draw needn't show every extreme that they name: `kept_bins`: 64 distinct bins in increasing order; both 1 and 255 are among them.
All inputs are finite; a program needn't handle non-finite values.
Results may differ from a plain program's by a relative error of at most 0.0003.
Values sent between devices are 32-bit elements; how exact they have to be, the bound alone decides.
A program may use at most 64 MiB of HBM per device.

v0:
```python
import math
import jax
import jax.numpy as jnp
from jax import lax
from jax.sharding import PartitionSpec as P

L = 512
HOP = 256
MODES = 4
ITERS = 3
precise = lax.Precision.HIGHEST


def make_table(kept_bins, block_len):
    offsets = jnp.arange(block_len, dtype=jnp.int32)
    phases = kept_bins[:, None] * offsets[None, :] % block_len
    angles = phases.astype(jnp.float32) * (2.0 * math.pi / block_len)
    window = (
        0.5 - 0.5 * jnp.cos(offsets.astype(jnp.float32) * (2.0 * math.pi / block_len))
    ) / math.sqrt(3.0 * block_len / 8.0)
    return jnp.stack([window * jnp.cos(angles), -window * jnp.sin(angles)])


def orthonormalize(w_real, w_imag):
    basis_re = []
    basis_im = []
    lengths = []
    for column in range(w_real.shape[-1]):
        orig_re = w_real[..., column]
        orig_im = w_imag[..., column]
        left_re = orig_re
        left_im = orig_im
        for earlier in range(column):
            prev_re = basis_re[earlier]
            prev_im = basis_im[earlier]
            coef_re = jnp.sum(prev_re * orig_re + prev_im * orig_im, axis=-1, keepdims=True)
            coef_im = jnp.sum(prev_re * orig_im - prev_im * orig_re, axis=-1, keepdims=True)
            left_re = left_re - (coef_re * prev_re - coef_im * prev_im)
            left_im = left_im - (coef_re * prev_im + coef_im * prev_re)
        length = jnp.sqrt(jnp.sum(left_re * left_re + left_im * left_im, axis=-1) + 1e-06)
        basis_re.append(left_re / length[..., None])
        basis_im.append(left_im / length[..., None])
        lengths.append(length)
    return (jnp.stack(basis_re, -1), jnp.stack(basis_im, -1), jnp.stack(lengths, -1))


def apply_gram(gram_re, gram_im, v_real, v_imag):
    pattern = "fbd,fdm->fbm"
    out_re = jnp.einsum(pattern, gram_re, v_real, precision=precise) - jnp.einsum(
        pattern, gram_im, v_imag, precision=precise
    )
    out_im = jnp.einsum(pattern, gram_re, v_imag, precision=precise) + jnp.einsum(
        pattern, gram_im, v_real, precision=precise
    )
    return (out_re, out_im)


def subspace(apply_fn, freq_count, block_count, mode_count):
    identity_cols = jnp.eye(block_count, mode_count, dtype=jnp.float32)
    v_real = jnp.broadcast_to(identity_cols, (freq_count, block_count, mode_count))
    v_imag = jnp.zeros((freq_count, block_count, mode_count), jnp.float32)
    lengths = jnp.zeros((freq_count, mode_count), jnp.float32)
    for sweep_step in range(ITERS):
        w_real, w_imag = apply_fn(v_real, v_imag)
        v_real, v_imag, lengths = orthonormalize(w_real, w_imag)
    return (v_real, v_imag, lengths)


def local_gram(x_real, x_imag, point_wts, norm_factor):
    y_real = x_real * point_wts
    y_imag = x_imag * point_wts
    pattern = "bfcp,dfcp->fbd"
    g_re = (
        jnp.einsum(pattern, y_real, x_real, precision=precise)
        + jnp.einsum(pattern, y_imag, x_imag, precision=precise)
    ) * norm_factor
    g_im = (
        jnp.einsum(pattern, y_real, x_imag, precision=precise)
        - jnp.einsum(pattern, y_imag, x_real, precision=precise)
    ) * norm_factor
    return (g_re, g_im)


def form_modes(x_real, x_imag, v_real, v_imag, lengths, block_count):
    pattern = "bfcp,fbm->fmcp"
    m_re = jnp.einsum(pattern, x_real, v_real, precision=precise) - jnp.einsum(
        pattern, x_imag, v_imag, precision=precise
    )
    m_im = jnp.einsum(pattern, x_real, v_imag, precision=precise) + jnp.einsum(
        pattern, x_imag, v_real, precision=precise
    )
    factor = (1.0 / jnp.sqrt(block_count * lengths))[:, :, None, None]
    return jnp.stack([m_re * factor, m_im * factor])


def total_gram(gram_parts):
    return lax.psum((gram_parts[0], gram_parts[1]), "sp")


def shards(snapshots, kept_bins, weights):
    dft_table = make_table(kept_bins, L)
    local_points = weights.shape[0]
    block_local = snapshots.shape[1] // HOP
    block_count = block_local * lax.axis_size("grp")
    norm_factor = 1.0 / (3.0 * local_points * lax.axis_size("sp"))
    regrouped = lax.all_to_all(snapshots, "grp", split_axis=2, concat_axis=1, tiled=True)
    sub_points = regrouped.shape[2]
    segments = regrouped.reshape(3, block_count, HOP, sub_points)
    following = jnp.roll(segments, -1, axis=1)
    blocks = jnp.concatenate([segments, following], axis=2)
    spectra = jnp.einsum("kft,cbtp->bkfcp", dft_table, blocks, precision=precise)
    x_real = spectra[:, 0]
    x_imag = spectra[:, 1]
    sub_wts = lax.dynamic_slice_in_dim(weights, lax.axis_index("grp") * sub_points, sub_points)
    g_re, g_im = local_gram(x_real, x_imag, sub_wts, norm_factor)
    g_re, g_im = (
        lax.psum_scatter(g_re, "grp", scatter_dimension=0, tiled=True),
        lax.psum_scatter(g_im, "grp", scatter_dimension=0, tiled=True),
    )
    g_re, g_im = total_gram((g_re, g_im))
    freq_count = g_re.shape[0]

    def apply_fn(v_real, v_imag):
        return apply_gram(g_re, g_im, v_real, v_imag)

    v_real, v_imag, lengths = subspace(apply_fn, freq_count, block_count, MODES)
    all_re, all_im, all_len = (
        lax.all_gather(v_real, "grp", axis=0, tiled=True),
        lax.all_gather(v_imag, "grp", axis=0, tiled=True),
        lax.all_gather(lengths, "grp", axis=0, tiled=True),
    )
    mode_fields = form_modes(x_real, x_imag, all_re, all_im, all_len, block_count)
    mode_fields = lax.all_to_all(mode_fields, "grp", split_axis=1, concat_axis=4, tiled=True)
    return (mode_fields, lengths)


def solution(mesh):
    in_specs = (P(None, "grp", "sp"), P(), P("sp"))
    out_specs = (P(None, "grp", None, None, "sp"), P("grp", None))
    return jax.shard_map(shards, mesh=mesh, in_specs=in_specs, out_specs=out_specs, check_vma=False)
```

profile of v0, /device:TPU:2, one launch (start us, length us, event | category | flops | bytes accessed | tf_op | source)
XLA Modules:
  0.0 621.5 jit_solution(10956544655818458053)
XLA Ops:
  7.2 7.4 %copy.333 = f32[3,1024,384]{1,0,2:T(4,128)} copy(f32[3,1024,384]{2,1,0:T(8,128)} %param.3) | data formatting | bytes 9437184 | tf_op args[0]
  14.6 7.2 %all-to-all-start = ((f32[3,1024,384]{1,0,2:T(4,128)}), f32[3,1024,384]{1,0,2:T(4,128)}, u32[]{:S(2)}, u32[]{:S(2)}) async-start(f32[3,1024,384]{1,0,2:T(4,128)} %copy.333), calls=%async_computation | async-start | bytes 12582912 | tf_op jit(solution)/shard_map/all_to_all | solution.py:106
  21.9 0.8 dynamic_slice.3
  22.7 0.6 cosine_multiply_fusion
  23.3 140.1 %all-to-all-done = f32[3,1024,384]{1,0,2:T(4,128)} async-done(((f32[3,1024,384]{1,0,2:T(4,128)}), f32[3,1024,384]{1,0,2:T(4,128)}, u32[]{:S(2)}, u32[]{:S(2)}) %all-to-all-start) | async-done | bytes 4718624 | tf_op jit(solution)/shard_map/all_to_all | solution.py:106
  163.3 5.5 copy.334
  168.8 4.9 copy.335
  173.7 6.5 %reshape.1735 = f32[3,32,256,48]{2,1,3,0:T(8,128)} reshape(f32[3,8,1024,48]{2,1,3,0:T(8,128)} %copy.335) | data formatting | bytes 9437184 | tf_op jit(solution)/shard_map/reshape | solution.py:108
  180.2 5.1 copy.338
  185.3 0.4 slice.114
  185.7 7.6 %fusion.5 = f32[32,2,64,3,48]{2,4,1,0,3:T(8,128)S(1)} fusion(f32[3,1,256,48]{2,3,1,0:T(8,128)S(1)} %slice.115, f32[3,31,256,48]{2,3,1,0:T(8,128)S(1)} %slice.114, f32[3,32,256,48]{2,3,1,0:T(8,128)S(1)} %copy.338, f32[1,64,512]{2,1,0:T(8,128)S(1)} %get-tuple-element.104, f32[1,64,512]{2,1,0:T(8,128)S(1)} %get-tuple-element.103), kind=kOutput, calls=%fused_computation.8 | convolution fusion | flops 3628662784 | bytes 12058624 | tf_op jit(solution)/shard_map/kft,cbtp->bkfcp/dot_general | solution.py:111
  193.4 1.9 slice_bitcast_fusion
  195.2 2.6 broadcast_multiply_fusion.1
  197.9 2.8 copy.343
  200.7 3.7 copy.340
  204.4 2.9 copy.341
  207.4 3.7 copy.342
  211.1 5.8 convolution_bitcast_fusion
  217.0 4.8 fusion.9
  221.8 0.4 reduce-scatter.3.cloned.1.call-start
  222.3 6.8 %convolution_bitcast_fusion.2 = f32[64,32,32]{2,1,0:T(8,128)S(1)} fusion(f32[32,64,3,48]{3,0,2,1:T(8,128)} %copy.342, f32[32,64,3,48]{3,0,2,1:T(8,128)} %copy.343), kind=kOutput, calls=%fused_computation.11 | convolution fusion | flops 113246208 | bytes 2621440 | tf_op jit(solution)/shard_map/bfcp,dfcp->fbd/dot_general | solution.py:75
  229.1 4.8 fusion.7
  234.0 28.4 %reduce-scatter.5.cloned.1.call-done = f32[8,32,32]{2,1,0:T(8,128)} async-done(((f32[64,32,32]{2,1,0:T(8,128)}), f32[8,32,32]{2,1,0:T(8,128)}) %reduce-scatter.5.cloned.1.call-update) | async-done | bytes 32784 | tf_op jit(solution)/shard_map/reduce_scatter | solution.py:118
  262.4 43.0 %reduce-scatter.3.cloned.1.call-done = f32[8,32,32]{2,1,0:T(8,128)} async-done(((f32[64,32,32]{2,1,0:T(8,128)}), f32[8,32,32]{2,1,0:T(8,128)}) %reduce-scatter.3.cloned.1.call-update) | async-done | bytes 32784 | tf_op jit(solution)/shard_map/reduce_scatter | solution.py:117
  305.4 188.0 %all-reduce.3.cloned.1.call-done = (f32[8,32,32]{2,1,0:T(8,128)}, f32[8,32,32]{2,1,0:T(8,128)}) async-done(((f32[8,32,32]{2,1,0:T(8,128)}, f32[8,32,32]{2,1,0:T(8,128)}), (f32[8,32,32]{2,1,0:T(8,128)}, f32[8,32,32]{2,1,0:T(8,128)})) %all-reduce.3.cloned.1.call-update) | async-done | bytes 65552 | tf_op jit(solution)/shard_map/psum | solution.py:97
  493.4 1.2 fusion.47
  494.6 1.2 fusion.49
  495.8 1.2 fusion.51
  497.1 1.2 fusion.45
  498.5 0.3 fusion.146
  498.9 0.2 fusion.130
  499.6 0.2 fusion.141
  500.0 1.2 fusion.37
  501.2 1.2 fusion.39
  502.4 1.2 fusion.41
  503.7 1.2 fusion.43
  505.0 0.3 fusion.110
  505.5 0.2 fusion.94
  505.7 0.2 add_reduce_fusion.2
  506.2 0.2 fusion.105
  506.5 1.2 fusion.35
  507.7 1.2 fusion.33
  509.0 1.2 fusion.29
  510.2 1.2 fusion.31
  511.6 0.3 fusion.74
  512.1 0.2 fusion.58
  512.7 0.2 fusion.69
  513.2 23.7 %all-gather = f32[8,8,4]{1,2,0:T(4,128)S(1)} all-gather(f32[1,8,4]{1,2,0:T(4,128)S(1)} %fusion.200), channel_id=1, replica_groups=mesh['grp'=8,'sp'=64] {'grp'}, dimensions={0}, use_global_device_ids=true | all-gather | bytes 1152 | tf_op jit(solution)/shard_map/all_gather | solution.py:130
  537.0 24.6 %all_gather.10 = f32[64,32,4]{1,2,0:T(4,128)S(1)} all-gather(f32[8,32,4]{1,2,0:T(4,128)S(1)} %copy.370), channel_id=1, replica_groups=mesh['grp'=8,'sp'=64] {'grp'}, dimensions={0}, use_global_device_ids=true | all-gather | bytes 36864 | tf_op jit(solution)/shard_map/all_gather | solution.py:129
  561.6 24.7 %all_gather.9 = f32[64,32,4]{1,2,0:T(4,128)S(1)} all-gather(f32[8,32,4]{1,2,0:T(4,128)S(1)} %copy.368), channel_id=1, replica_groups=mesh['grp'=8,'sp'=64] {'grp'}, dimensions={0}, use_global_device_ids=true | all-gather | bytes 36864 | tf_op jit(solution)/shard_map/all_gather | solution.py:128
  586.3 1.9 fusion.20
  588.2 1.9 fusion.22
  590.2 1.9 fusion.11
  592.1 1.9 fusion.13
  594.0 0.2 copy_bitcast_fusion
  594.3 1.6 reshape.1749
  595.8 3.9 all-to-all-start.1
  599.7 0.6 pad_maximum_fusion.7
  600.3 10.2 %all-to-all-done.1 = f32[8,1,9216]{2,1,0:T(1,128)S(1)} async-done(((f32[8,1,9216]{2,1,0:T(1,128)}), f32[8,1,9216]{2,1,0:T(1,128)S(1)}, u32[]{:S(2)}, u32[]{:S(2)}) %all-to-all-start.1) | async-done | bytes 294944 | tf_op jit(solution)/shard_map/all_to_all | solution.py:133
  610.6 0.5 broadcast.1517
  611.1 1.3 reduce
  612.4 0.8 reshape.1750
  613.3 0.5 copy.377
  613.7 1.1 all_to_all.30
  (64 shorter events, 3.0 us)
Async XLA Ops:
  14.6 8.1 %copy-start.4 = (s32[64]{0:T(128)S(1)}, s32[64]{0:T(128)}, u32[]{:S(2)}) copy-start(s32[64]{0:T(128)} %param.4) | copy-start | bytes 772
  14.6 148.8 %all-to-all-start = ((f32[3,1024,384]{1,0,2:T(4,128)}), f32[3,1024,384]{1,0,2:T(4,128)}, u32[]{:S(2)}, u32[]{:S(2)}) async-start(f32[3,1024,384]{1,0,2:T(4,128)} %copy.333), calls=%async_computation | async-start | bytes 12582912 | tf_op jit(solution)/shard_map/all_to_all | solution.py:106
  21.8 240.6 %reduce-scatter.5.cloned.1.call-start = ((), (), s32[]{:S(2)}) async-start(), calls=%async_computation.5 | async-start | bytes 1179648 | tf_op jit(solution)/shard_map/reduce_scatter | solution.py:118
  211.1 5.9 copy-start
  211.1 5.9 copy-start.2
  221.8 83.6 %reduce-scatter.3.cloned.1.call-start = ((), (), s32[]{:S(2)}) async-start(), calls=%async_computation.4 | async-start | bytes 1179648 | tf_op jit(solution)/shard_map/reduce_scatter | solution.py:117
  222.3 6.8 %copy-start.3 = (f32[32,64,3,48]{3,0,2,1:T(8,128)S(1)}, f32[32,64,3,48]{3,0,2,1:T(8,128)}, u32[]{:S(2)}) copy-start(f32[32,64,3,48]{3,0,2,1:T(8,128)} %copy.340) | copy-start | bytes 3538948
  233.9 259.5 %all-reduce.3.cloned.1.call-start = ((), (), s32[]{:S(2)}) async-start(), calls=%async_computation.6 | async-start | bytes 524288 | tf_op jit(solution)/shard_map/psum | solution.py:97
  586.3 3.8 copy-start.1
  595.8 14.7 %all-to-all-start.1 = ((f32[8,1,9216]{2,1,0:T(1,128)}), f32[8,1,9216]{2,1,0:T(1,128)S(1)}, u32[]{:S(2)}, u32[]{:S(2)}) async-start(f32[8,1,9216]{2,1,0:T(1,128)} %reshape.1749), calls=%async_computation.3 | async-start | bytes 589824 | tf_op jit(solution)/shard_map/all_to_all | solution.py:133
Sparse Core Ops, SparseCore 0:
  221.9 40.4 reduce-scatter.4
  265.2 40.1 reduce-scatter.2
  308.9 184.4 all-reduce.2
where the time goes:
time: 628 us; the launch traced here: 622 us
  waiting for transfers between devices  410 us (65%)
  blocking collectives  73 us (12%)
  matrix products  52.3 us (8%)
  local copies, waits for them, and re-layouts  50.2 us (8%)
  between operations  14.3 us (2%)
  starting transfers between devices  11.7 us (2%)
  other arithmetic  10.3 us (2%)
    psum x1, waiting for transfers between devices, total_gram(): return lax.psum((gram_parts[0], gram_parts[1]), 'sp')  188 us
    all_to_all x1, waiting for transfers between devices, shards(): lax.all_to_all(snapshots, 'grp', split_axis=2, concat_axis=1, tiled=True)  140 us
    reduce_scatter x1, waiting for transfers between devices, shards(): lax.psum_scatter(g_re, 'grp', scatter_dimension=0, tiled=True)  43 us
    reduce_scatter x1, waiting for transfers between devices, shards(): lax.psum_scatter(g_im, 'grp', scatter_dimension=0, tiled=True)  28.4 us
    all_gather x1, blocking collectives, shards(): lax.all_gather(v_real, 'grp', axis=0, tiled=True)  24.7 us
    all_gather x1, blocking collectives, shards(): lax.all_gather(v_imag, 'grp', axis=0, tiled=True)  24.6 us
    all_gather x1, blocking collectives, shards(): lax.all_gather(lengths, 'grp', axis=0, tiled=True)  23.7 us
  transfers between devices with their start and end apart: 5, of which 5 were waited for; matrix products, arithmetic and copies ran while one was open for 2% of the time, Pallas kernels for 0%

commit v1 on v0

--- a/solution.py
+++ b/solution.py
@@ -126,7 +126,15 @@
     v_real, v_imag, lengths = subspace(apply_fn, freq_count, block_count, MODES)
     all_re, all_im, all_len = (
         lax.all_gather(v_real, "grp", axis=0, tiled=True),
-        lax.all_gather(v_imag, "grp", axis=0, tiled=True),
+        jnp.concatenate(
+            lax.all_to_all(
+                jnp.stack(lax.axis_size("grp") * [v_imag], 0),
+                axis_name="grp",
+                split_axis=0,
+                concat_axis=0,
+            ),
+            0,
+        ),
         lax.all_gather(lengths, "grp", axis=0, tiled=True),
     )
     mode_fields = form_modes(x_real, x_imag, all_re, all_im, all_len, block_count)

time: 628 us -> 623 us (level)
  blocking collectives: 73 us -> 51.8 us
    all_gather x1 -> x0, blocking collectives: 24.6 us -> none  [shards(): lax.all_gather(v_imag, 'grp', axis=0, tiled=True)]
  transfers between devices with their start and end apart: 5 -> 6, of which waited for: 5 -> 6; matrix products, arithmetic and copies ran while one was open for 2% -> 3% of each run, Pallas kernels for 0% -> 0%
where the time goes in v1:
time: 623 us; the launch traced here: 616 us
  waiting for transfers between devices  414 us (66%)
  matrix products  54.3 us (9%)
  local copies, waits for them, and re-layouts  53.3 us (9%)
  blocking collectives  51.8 us (8%)
  starting transfers between devices  15.7 us (3%)
  between operations  14.5 us (2%)
  other arithmetic  12.3 us (2%)
    psum x1, waiting for transfers between devices, total_gram(): return lax.psum((gram_parts[0], gram_parts[1]), 'sp')  188 us
    all_to_all x1, waiting for transfers between devices, shards(): lax.all_to_all(snapshots, 'grp', split_axis=2, concat_axis=1, tiled=True)  140 us
    reduce_scatter x1, waiting for transfers between devices, shards(): lax.psum_scatter(g_re, 'grp', scatter_dimension=0, tiled=True)  43 us
    reduce_scatter x1, waiting for transfers between devices, shards(): lax.psum_scatter(g_im, 'grp', scatter_dimension=0, tiled=True)  28.4 us
    all_gather x1, blocking collectives, shards(): lax.all_gather(v_real, 'grp', axis=0, tiled=True)  26.6 us
    all_gather x1, blocking collectives, shards(): lax.all_gather(lengths, 'grp', axis=0, tiled=True)  25.1 us
  transfers between devices with their start and end apart: 6, of which 6 were waited for; matrix products, arithmetic and copies ran while one was open for 3% of the time, Pallas kernels for 0%

profile of v1, /device:TPU:2, one launch (start us, length us, event | category | flops | bytes accessed | tf_op | source)
XLA Modules:
  0.0 616.0 jit_solution(14817924703017297112)
XLA Ops:
  7.2 7.4 %copy.333 = f32[3,1024,384]{1,0,2:T(4,128)} copy(f32[3,1024,384]{2,1,0:T(8,128)} %param.3) | data formatting | bytes 9437184 | tf_op args[0]
  14.6 7.2 %all-to-all-start = ((f32[3,1024,384]{1,0,2:T(4,128)}), f32[3,1024,384]{1,0,2:T(4,128)}, u32[]{:S(2)}, u32[]{:S(2)}) async-start(f32[3,1024,384]{1,0,2:T(4,128)} %copy.333), calls=%async_computation | async-start | bytes 12582912 | tf_op jit(solution)/shard_map/all_to_all | solution.py:106
  21.9 0.8 dynamic_slice.3
  22.7 0.6 cosine_multiply_fusion
  23.3 140.1 %all-to-all-done = f32[3,1024,384]{1,0,2:T(4,128)} async-done(((f32[3,1024,384]{1,0,2:T(4,128)}), f32[3,1024,384]{1,0,2:T(4,128)}, u32[]{:S(2)}, u32[]{:S(2)}) %all-to-all-start) | async-done | bytes 4718624 | tf_op jit(solution)/shard_map/all_to_all | solution.py:106
  163.3 5.5 copy.334
  168.8 4.9 copy.335
  173.7 6.5 %reshape.1740 = f32[3,32,256,48]{2,1,3,0:T(8,128)} reshape(f32[3,8,1024,48]{2,1,3,0:T(8,128)} %copy.335) | data formatting | bytes 9437184 | tf_op jit(solution)/shard_map/reshape | solution.py:108
  180.2 5.1 copy.338
  185.3 0.4 slice.114
  185.7 7.6 %fusion.5 = f32[32,2,64,3,48]{2,4,1,0,3:T(8,128)S(1)} fusion(f32[3,1,256,48]{2,3,1,0:T(8,128)S(1)} %slice.115, f32[3,31,256,48]{2,3,1,0:T(8,128)S(1)} %slice.114, f32[3,32,256,48]{2,3,1,0:T(8,128)S(1)} %copy.338, f32[1,64,512]{2,1,0:T(8,128)S(1)} %get-tuple-element.104, f32[1,64,512]{2,1,0:T(8,128)S(1)} %get-tuple-element.103), kind=kOutput, calls=%fused_computation.8 | convolution fusion | flops 3628662784 | bytes 12058624 | tf_op jit(solution)/shard_map/kft,cbtp->bkfcp/dot_general | solution.py:111
  193.4 1.9 slice_bitcast_fusion
  195.3 2.7 broadcast_multiply_fusion.1
  198.0 2.8 copy.343
  200.8 3.7 copy.340
  204.6 2.9 copy.341
  207.5 3.7 copy.342
  211.2 5.8 convolution_bitcast_fusion
  217.1 4.8 fusion.9
  222.0 0.4 reduce-scatter.3.cloned.1.call-start
  222.4 6.8 %convolution_bitcast_fusion.2 = f32[64,32,32]{2,1,0:T(8,128)S(1)} fusion(f32[32,64,3,48]{3,0,2,1:T(8,128)} %copy.342, f32[32,64,3,48]{3,0,2,1:T(8,128)} %copy.343), kind=kOutput, calls=%fused_computation.11 | convolution fusion | flops 113246208 | bytes 2621440 | tf_op jit(solution)/shard_map/bfcp,dfcp->fbd/dot_general | solution.py:75
  229.2 4.8 fusion.7
  234.2 28.4 %reduce-scatter.5.cloned.1.call-done = f32[8,32,32]{2,1,0:T(8,128)} async-done(((f32[64,32,32]{2,1,0:T(8,128)}), f32[8,32,32]{2,1,0:T(8,128)}) %reduce-scatter.5.cloned.1.call-update) | async-done | bytes 32784 | tf_op jit(solution)/shard_map/reduce_scatter | solution.py:118
  262.5 43.0 %reduce-scatter.3.cloned.1.call-done = f32[8,32,32]{2,1,0:T(8,128)} async-done(((f32[64,32,32]{2,1,0:T(8,128)}), f32[8,32,32]{2,1,0:T(8,128)}) %reduce-scatter.3.cloned.1.call-update) | async-done | bytes 32784 | tf_op jit(solution)/shard_map/reduce_scatter | solution.py:117
  305.6 188.1 %all-reduce.3.cloned.1.call-done = (f32[8,32,32]{2,1,0:T(8,128)}, f32[8,32,32]{2,1,0:T(8,128)}) async-done(((f32[8,32,32]{2,1,0:T(8,128)}, f32[8,32,32]{2,1,0:T(8,128)}), (f32[8,32,32]{2,1,0:T(8,128)}, f32[8,32,32]{2,1,0:T(8,128)})) %all-reduce.3.cloned.1.call-update) | async-done | bytes 65552 | tf_op jit(solution)/shard_map/psum | solution.py:97
  493.6 1.2 fusion.44
  494.8 1.2 fusion.46
  496.1 1.2 fusion.48
  497.3 1.2 fusion.42
  498.7 0.3 fusion.143
  499.1 0.2 fusion.127
  500.2 1.2 fusion.34
  501.4 1.2 fusion.36
  502.7 1.2 fusion.38
  503.9 1.2 fusion.40
  505.3 0.3 fusion.107
  505.7 0.2 fusion.91
  506.7 1.2 fusion.32
  507.9 1.2 fusion.30
  509.2 1.2 fusion.26
  510.5 1.2 fusion.28
  511.9 0.3 fusion.71
  512.3 0.2 fusion.55
  513.4 25.1 %all-gather = f32[8,8,4]{1,2,0:T(4,128)} all-gather(f32[1,8,4]{1,2,0:T(4,128)S(1)} %fusion.200), channel_id=1, replica_groups=mesh['grp'=8,'sp'=64] {'grp'}, dimensions={0}, use_global_device_ids=true | all-gather | bytes 1152 | tf_op jit(solution)/shard_map/all_gather | solution.py:138
  538.6 26.6 %all_gather.6 = f32[64,32,4]{1,2,0:T(4,128)} all-gather(f32[8,32,4]{1,2,0:T(4,128)S(1)} %copy.368), channel_id=1, replica_groups=mesh['grp'=8,'sp'=64] {'grp'}, dimensions={0}, use_global_device_ids=true | all-gather | bytes 36864 | tf_op jit(solution)/shard_map/all_gather | solution.py:128
  565.3 0.8 reshape.1755
  566.0 4.4 all-to-all-start.1
  570.4 2.8 fusion.20
  573.2 0.7 copy.386
  573.9 4.6 all-to-all-done.1
  578.5 0.5 broadcast.1519
  579.0 2.0 reduce
  581.0 1.5 reshape.1756
  582.6 3.0 fusion.173
  585.5 1.9 fusion.13
  587.5 1.9 fusion.11
  589.7 1.6 reshape.1757
  591.3 3.6 all-to-all-start.2
  594.9 0.6 pad_maximum_fusion.7
  595.5 10.1 %all-to-all-done.2 = f32[8,1,9216]{2,1,0:T(1,128)S(1)} async-done(((f32[8,1,9216]{2,1,0:T(1,128)}), f32[8,1,9216]{2,1,0:T(1,128)S(1)}, u32[]{:S(2)}, u32[]{:S(2)}) %all-to-all-start.2) | async-done | bytes 294944 | tf_op jit(solution)/shard_map/all_to_all | solution.py:141
  605.6 1.3 reduce.1
  606.9 0.8 reshape.1758
  607.8 0.5 copy.377
  608.2 1.1 all_to_all.34
  (93 shorter events, 3.9 us)
Async XLA Ops:
  14.6 8.1 %copy-start.16 = (s32[64]{0:T(128)S(1)}, s32[64]{0:T(128)}, u32[]{:S(2)}) copy-start(s32[64]{0:T(128)} %param.4) | copy-start | bytes 772
  14.6 148.8 %all-to-all-start = ((f32[3,1024,384]{1,0,2:T(4,128)}), f32[3,1024,384]{1,0,2:T(4,128)}, u32[]{:S(2)}, u32[]{:S(2)}) async-start(f32[3,1024,384]{1,0,2:T(4,128)} %copy.333), calls=%async_computation | async-start | bytes 12582912 | tf_op jit(solution)/shard_map/all_to_all | solution.py:106
  21.8 240.7 %reduce-scatter.5.cloned.1.call-start = ((), (), s32[]{:S(2)}) async-start(), calls=%async_computation.6 | async-start | bytes 1179648 | tf_op jit(solution)/shard_map/reduce_scatter | solution.py:118
  211.2 5.9 copy-start
  211.2 5.9 copy-start.2
  222.0 83.6 %reduce-scatter.3.cloned.1.call-start = ((), (), s32[]{:S(2)}) async-start(), calls=%async_computation.5 | async-start | bytes 1179648 | tf_op jit(solution)/shard_map/reduce_scatter | solution.py:117
  222.4 6.8 %copy-start.3 = (f32[32,64,3,48]{3,0,2,1:T(8,128)S(1)}, f32[32,64,3,48]{3,0,2,1:T(8,128)}, u32[]{:S(2)}) copy-start(f32[32,64,3,48]{3,0,2,1:T(8,128)} %copy.340) | copy-start | bytes 3538948
  234.1 259.5 %all-reduce.3.cloned.1.call-start = ((), (), s32[]{:S(2)}) async-start(), calls=%async_computation.7 | async-start | bytes 524288 | tf_op jit(solution)/shard_map/psum | solution.py:97
  511.8 53.4 %copy-start.8 = (f32[8,1]{0,1:T(1,128)}, f32[8,1]{0,1:T(1,128)S(1)}, u32[]{:S(2)}) copy-start(f32[8,1]{0,1:T(1,128)S(1)} %get-tuple-element.95) | copy-start | bytes 100
  512.3 52.9 %copy-start.10 = (f32[8,1]{0,1:T(1,128)}, f32[8,1]{0,1:T(1,128)S(1)}, u32[]{:S(2)}) copy-start(f32[8,1]{0,1:T(1,128)S(1)} %get-tuple-element.97) | copy-start | bytes 100
  512.8 52.4 %copy-start.12 = (f32[8,1]{0,1:T(1,128)}, f32[8,1]{0,1:T(1,128)S(1)}, u32[]{:S(2)}) copy-start(f32[8,1]{0,1:T(1,128)S(1)} %get-tuple-element.99) | copy-start | bytes 100
  513.2 52.0 %copy-start.14 = (f32[8,1]{0,1:T(1,128)}, f32[8,1]{0,1:T(1,128)S(1)}, u32[]{:S(2)}) copy-start(f32[8,1]{0,1:T(1,128)S(1)} %get-tuple-element.101) | copy-start | bytes 100
  566.0 12.5 %all-to-all-start.1 = ((f32[8,1,1024]{2,1,0:T(1,128)}), f32[8,1,1024]{2,1,0:T(1,128)}, u32[]{:S(2)}, u32[]{:S(2)}) async-start(f32[8,1,1024]{2,1,0:T(1,128)} %reshape.1755), calls=%async_computation.3 | async-start | bytes 65536 | tf_op jit(solution)/shard_map/all_to_all | solution.py:130
  570.4 2.8 copy-start.7
  582.5 3.0 copy-start.1
  582.5 3.0 copy-start.5
  582.5 3.0 copy-start.6
  582.5 4.9 copy-start.4
  587.5 7.4 %copy-start.9 = (f32[8,1]{0,1:T(1,128)S(1)}, f32[8,1]{0,1:T(1,128)}, u32[]{:S(2)}) copy-start(f32[8,1]{0,1:T(1,128)} %copy-done.8) | copy-start | bytes 100
  587.5 7.4 %copy-start.11 = (f32[8,1]{0,1:T(1,128)S(1)}, f32[8,1]{0,1:T(1,128)}, u32[]{:S(2)}) copy-start(f32[8,1]{0,1:T(1,128)} %copy-done.10) | copy-start | bytes 100
  587.5 7.4 %copy-start.13 = (f32[8,1]{0,1:T(1,128)S(1)}, f32[8,1]{0,1:T(1,128)}, u32[]{:S(2)}) copy-start(f32[8,1]{0,1:T(1,128)} %copy-done.12) | copy-start | bytes 100
  587.5 7.4 %copy-start.15 = (f32[8,1]{0,1:T(1,128)S(1)}, f32[8,1]{0,1:T(1,128)}, u32[]{:S(2)}) copy-start(f32[8,1]{0,1:T(1,128)} %copy-done.14) | copy-start | bytes 100
  591.3 14.4 %all-to-all-start.2 = ((f32[8,1,9216]{2,1,0:T(1,128)}), f32[8,1,9216]{2,1,0:T(1,128)S(1)}, u32[]{:S(2)}, u32[]{:S(2)}) async-start(f32[8,1,9216]{2,1,0:T(1,128)} %reshape.1757), calls=%async_computation.4 | async-start | bytes 589824 | tf_op jit(solution)/shard_map/all_to_all | solution.py:141
Sparse Core Ops, SparseCore 0:
  222.1 40.4 reduce-scatter.4
  265.4 40.1 reduce-scatter.2
  309.1 184.4 all-reduce.2
